TPU v7x, 256 devices: a whole 4x4x8 slice. The times are simulated.
256 devices in a mesh: row: 4 (over y), col: 32 (over x_lo, z, core), feat: 2 (over x_hi).
Axes of the slice: x: 4 (x_hi: 2, x_lo: 2; x = x_hi * 2 + x_lo), y: 4, z: 8, core: 2. Of those that a mesh axis runs over, the one named last changes fastest.
Arguments:
- panel_student: bfloat16 [2048, 4096], P('row', 'feat'), may hold values from -0.01171875 to 0.01171875
- panel_teacher: bfloat16 [2048, 4096], P('row', 'feat'), may hold values from -0.01171875 to 0.01171875
- tokens_student: bfloat16 [24576, 4096], P('col', 'feat'), may hold values from -0.01171875 to 0.01171875
- tokens_teacher: bfloat16 [24576, 4096], P('col', 'feat'), may hold values from -0.01171875 to 0.01171875
Outputs:
- row_loss: float32 [2048], P(('row', 'col'))
- grad_panel: bfloat16 [2048, 4096], P(('row', 'col'), 'feat')
- grad_tokens: bfloat16 [24576, 4096], P('col', 'feat')
All inputs are finite; a program needn't handle non-finite values.
Results may differ from a plain program's by a relative error of at most 0.0058.
Values may be sent and summed in bfloat16 or wider, within the bound.
No kernel may reach another device: no remote copies, remote signals or barrier semaphores. Data moves between devices by JAX's collectives and lax.ppermute only.
A program may use at most 128 MiB of HBM per device.

v0:
```python
import jax
import jax.numpy as jnp
from jax import lax
from jax.sharding import PartitionSpec as P

epsilon = 1e-06


def squares(features):
    values = features.astype(jnp.float32)
    return jnp.sum(values * values, axis=1)


def inner(left, right):
    return jnp.einsum("rd,cd->rc", left, right, preferred_element_type=jnp.float32)


def inverse(total):
    return 1.0 / jnp.sqrt(total + epsilon)


def local(panel_student, panel_teacher, tokens_student, tokens_teacher):
    student_dots, teacher_dots, sq_ps, sq_pt, sq_ts, sq_tt = lax.psum(
        (
            inner(panel_student, tokens_student),
            inner(panel_teacher, tokens_teacher),
            squares(panel_student),
            squares(panel_teacher),
            squares(tokens_student),
            squares(tokens_teacher),
        ),
        "feat",
    )
    inv_ps = inverse(sq_ps)
    inv_pt = inverse(sq_pt)
    inv_ts = inverse(sq_ts)
    inv_tt = inverse(sq_tt)
    student_gram = student_dots * inv_ps[:, None] * inv_ts[None, :]
    teacher_gram = teacher_dots * inv_pt[:, None] * inv_tt[None, :]
    mismatch = student_gram - teacher_gram
    loss_part = jnp.sum(mismatch * mismatch, axis=1)
    doubled = (2.0 * mismatch).astype(jnp.bfloat16)
    panel_unit = panel_student.astype(jnp.float32) * inv_ps[:, None]
    token_unit = tokens_student.astype(jnp.float32) * inv_ts[:, None]
    panel_half = panel_unit.astype(jnp.bfloat16)
    token_half = token_unit.astype(jnp.bfloat16)
    panel_part = jnp.dot(doubled, token_half, preferred_element_type=jnp.float32)
    panel_term, row_loss = (
        lax.psum_scatter(panel_part, "col", scatter_dimension=0, tiled=True),
        lax.psum_scatter(loss_part, "col", scatter_dimension=0, tiled=True),
    )
    token_part = jnp.einsum("rc,rd->cd", doubled, panel_half, preferred_element_type=jnp.float32)
    token_term = lax.psum(token_part, "row")
    share = panel_student.shape[0] // lax.axis_size("col")
    offset = lax.axis_index("col") * share
    unit_rows = lax.dynamic_slice_in_dim(panel_unit, offset, share, 0)
    inv_rows = lax.dynamic_slice_in_dim(inv_ps, offset, share, 0)
    along_panel, along_tokens = lax.psum(
        (jnp.sum(unit_rows * panel_term, axis=1), jnp.sum(token_unit * token_term, axis=1)), "feat"
    )
    grad_panel = ((panel_term - unit_rows * along_panel[:, None]) * inv_rows[:, None]).astype(
        jnp.bfloat16
    )
    grad_tokens = ((token_term - token_unit * along_tokens[:, None]) * inv_ts[:, None]).astype(
        jnp.bfloat16
    )
    return (row_loss, grad_panel, grad_tokens)


def solution(mesh):
    placed = (P("row", "feat"), P("row", "feat"), P("col", "feat"), P("col", "feat"))
    return jax.shard_map(
        local,
        mesh=mesh,
        in_specs=placed,
        out_specs=(P(("row", "col")), P(("row", "col"), "feat"), P("col", "feat")),
        check_vma=False,
    )
```

profile of v0, /device:TPU:8, one launch (start us, length us, event | category | flops | bytes accessed | tf_op | source)
XLA Modules:
  0.0 405.1 jit_solution(3159031561422616562)
XLA Ops:
  7.2 0.0 copy-start
  7.2 0.0 all-reduce.9.cloned.1.call-start
  7.2 0.0 copy-start.1
  7.2 5.7 %fusion.17 = f32[512,768]{1,0:T(8,128)} fusion(bf16[512,2048]{1,0:T(8,128)(2,1)} %param.5, bf16[768,2048]{1,0:T(8,128)(2,1)} %param.7), kind=kOutput, calls=%fused_computation.31 | convolution fusion | flops 1610612736 | bytes 6815744 | tf_op jit(solution)/shard_map/rd,cd->rc/dot_general | solution.py:15
  12.9 0.0 copy-done
  12.9 0.0 copy-done.1
  12.9 3.1 fusion.16
  15.9 0.0 all-reduce.9.cloned.1.call-update
  16.0 0.0 all-reduce.7.cloned.1.call-start
  16.0 0.0 copy-start.2
  16.0 2.2 multiply_reduce_fusion.1
  18.3 0.0 copy-done.2
  18.3 0.5 fusion.8
  18.7 2.6 multiply_reduce_fusion
  21.3 0.7 fusion.7
  22.0 11.1 %all-reduce.2 = (f32[768]{0:T(1024)S(1)}, f32[512]{0:T(512)S(1)}, f32[768]{0:T(1024)S(1)}, f32[512]{0:T(512)S(1)}) all-reduce(f32[768]{0:T(1024)S(1)} %multiply_reduce_fusion, f32[512]{0:T(512)S(1)} %multiply_reduce_fusion.1, f32[768]{0:T(1024)S(1)} %fusion.7, f32[512]{0:T(512)S(1)} %fusion.8), channel_id=1, replica_groups=mesh['row'=4,'col'=32,'feat'=2] {'feat'}, use_global_device_ids=true, to_apply=%region_9.0 | all-reduce | flops 2560 | bytes 20480 | tf_op jit(solution)/shard_map/psum | solution.py:23
  33.1 85.0 %all-reduce.9.cloned.1.call-done = (f32[512,768]{1,0:T(8,128)}, f32[512,768]{1,0:T(8,128)}) async-done(((f32[512,768]{1,0:T(8,128)}, f32[512,768]{1,0:T(8,128)}), (f32[512,768]{1,0:T(8,128)}, f32[512,768]{1,0:T(8,128)})) %all-reduce.9.cloned.1.call-update) | async-done | bytes 3145744 | tf_op jit(solution)/shard_map/psum | solution.py:23
  118.1 0.0 copy-start.3
  118.1 2.6 multiply_reduce_fusion.2
  120.8 0.0 copy-start.4
  120.8 1.1 copy-done.4
  121.9 0.0 copy-done.3
  121.9 4.6 %fusion.12 = f32[768,2048]{1,0:T(8,128)} fusion(f32[512,768]{1,0:T(8,128)S(1)} %get-tuple-element.12, bf16[512,2048]{1,0:T(8,128)(2,1)S(1)} %copy-done.3, f32[512]{0:T(512)S(1)} %get-tuple-element.16), kind=kOutput, calls=%fused_computation.17 | convolution fusion | flops 1614544896 | bytes 9963520 | tf_op jit(solution)/shard_map/rc,rd->cd/dot_general | solution.py:52
  126.5 0.0 all-reduce.7.cloned.1.call-update
  126.5 0.0 reduce-scatter.2.cloned.1.call-start
  126.6 5.2 %fusion.9 = f32[512,2048]{1,0:T(8,128)} fusion(bf16[768,2048]{1,0:T(8,128)(2,1)S(1)} %copy-done, f32[768]{0:T(1024)S(1)} %get-tuple-element.14, f32[512,768]{1,0:T(8,128)} %copy-done.4), kind=kOutput, calls=%fused_computation.15 | convolution fusion | flops 1616117760 | bytes 8915968 | tf_op jit(solution)/shard_map/dot_general | solution.py:47
  131.8 0.0 copy-start.6
  131.8 0.0 reduce-scatter.2.cloned.1.call-update
  131.9 0.1 dynamic_slice.7
  131.9 0.6 copy-done.6
  132.5 0.6 dynamic-slice
  133.7 4.4 %convert_multiply_fusion.2 = f32[512,2048]{1,0:T(8,128)} fusion(bf16[512,2048]{1,0:T(8,128)(2,1)} %param.4, f32[512]{0:T(512)S(1)} %get-tuple-element.16), kind=kLoop, calls=%fused_computation.11 | loop fusion | flops 2097152 | bytes 6293504 | tf_op jit(solution)/shard_map/mul | solution.py:43
  138.2 55.0 %all-reduce = f32[512]{0:T(512)S(1)} all-reduce(f32[512]{0:T(512)S(1)} %get-tuple-element.11), channel_id=2, replica_groups=mesh['row'=4,'col'=32,'feat'=2] {'col'}, use_global_device_ids=true, to_apply=%region_11.0.clone | all-reduce | flops 512 | bytes 4096
  193.2 0.6 dynamic-slice.1
  193.8 63.3 %all-reduce.7.cloned.1.call-done = f32[768,2048]{1,0:T(8,128)} async-done(((f32[768,2048]{1,0:T(8,128)}), f32[768,2048]{1,0:T(8,128)}) %all-reduce.7.cloned.1.call-update) | async-done | bytes 6291472 | tf_op jit(solution)/shard_map/psum | solution.py:53
  257.1 3.7 fusion.3
  260.9 123.8 %reduce-scatter.2.cloned.1.call-done = f32[16,2048]{1,0:T(8,128)} async-done(((f32[512,2048]{1,0:T(8,128)}), f32[16,2048]{1,0:T(8,128)}) %reduce-scatter.2.cloned.1.call-update) | async-done | bytes 131088 | tf_op jit(solution)/shard_map/reduce_scatter | solution.py:49
  384.7 1.1 multiply_reduce_fusion.3
  385.8 6.5 %all-reduce.1 = (f32[16]{0:T(128)S(1)}, f32[768]{0:T(1024)S(1)}) all-reduce(f32[16]{0:T(128)S(1)} %multiply_reduce_fusion.3, f32[768]{0:T(1024)S(1)} %fusion.3), channel_id=1, replica_groups=mesh['row'=4,'col'=32,'feat'=2] {'feat'}, use_global_device_ids=true, to_apply=%region_14.0 | all-reduce | flops 784 | bytes 6272 | tf_op jit(solution)/shard_map/psum | solution.py:58
  392.3 0.0 copy-start.5
  392.3 4.7 %fusion.6 = bf16[768,2048]{1,0:T(8,128)(2,1)} fusion(f32[768,2048]{1,0:T(8,128)} %all-reduce.7.cloned.1.call-done, bf16[768,2048]{1,0:T(8,128)(2,1)S(1)} %copy-done, f32[768]{0:T(1024)S(1)} %get-tuple-element.4, f32[768]{0:T(1024)S(1)} %get-tuple-element.14), kind=kLoop, calls=%fused_computation.8 | loop fusion | flops 9437184 | bytes 12589056 | tf_op jit(solution)/shard_map/convert_element_type | solution.py:64
  397.0 0.0 copy-done.5
  397.0 1.6 multiply_convert_fusion.3
  (2 shorter events, 0.0 us)
Async XLA Ops:
  7.2 5.7 %copy-start = (bf16[768,2048]{1,0:T(8,128)(2,1)S(1)}, bf16[768,2048]{1,0:T(8,128)(2,1)}, u32[]{:S(2)}) copy-start(bf16[768,2048]{1,0:T(8,128)(2,1)} %param.6) | copy-start | bytes 9437188
  7.2 111.0 %all-reduce.9.cloned.1.call-start = ((), (), s32[]{:S(2)}) async-start(), calls=%async_computation.3 | async-start | bytes 6291456 | tf_op jit(solution)/shard_map/psum | solution.py:23
  7.2 5.7 %copy-start.1 = (bf16[512,2048]{1,0:T(8,128)(2,1)S(1)}, bf16[512,2048]{1,0:T(8,128)(2,1)}, u32[]{:S(2)}) copy-start(bf16[512,2048]{1,0:T(8,128)(2,1)} %param.4) | copy-start | bytes 6291460
  16.0 241.1 %all-reduce.7.cloned.1.call-start = ((), (), s32[]{:S(2)}) async-start(), calls=%async_computation.2 | async-start | bytes 12582912 | tf_op jit(solution)/shard_map/psum | solution.py:53
  16.0 2.2 copy-start.2
  118.1 3.8 copy-start.3
  120.8 1.1 copy-start.4
  126.5 258.1 %reduce-scatter.2.cloned.1.call-start = ((), (), s32[]{:S(2)}) async-start(), calls=%async_computation.1 | async-start | bytes 4325376 | tf_op jit(solution)/shard_map/reduce_scatter | solution.py:49
  131.8 0.7 copy-start.6
  392.3 4.7 %copy-start.5 = (f32[16,2048]{1,0:T(8,128)S(1)}, f32[16,2048]{1,0:T(8,128)}, u32[]{:S(2)}) copy-start(f32[16,2048]{1,0:T(8,128)} %reduce-scatter.2.cloned.1.call-done) | copy-start | bytes 393220
Sparse Core Ops, SparseCore 0:
  16.1 101.9 all-reduce.8
  126.7 130.4 all-reduce.6
  259.7 124.9 reduce-scatter.1
where the time goes:
time: 405 us
  waiting for transfers between devices  272 us (67%)
  blocking collectives  72.6 us (18%)
  other arithmetic  24.2 us (6%)
  matrix products  18.5 us (5%)
  between operations  14.5 us (4%)
    reduce_scatter x1, waiting for transfers between devices, local(): lax.psum_scatter(panel_part, 'col', scatter_dimension=0, tiled=True)  124 us
    psum x1, waiting for transfers between devices, local(): lax.psum((inner(panel_student, tokens_student), inner(panel_teacher, toke...  85 us
    psum x1, waiting for transfers between devices, local(): token_term = lax.psum(token_part, 'row')  63.3 us
    unnamed x1, blocking collectives  55 us
    psum x1, blocking collectives, local(): lax.psum((inner(panel_student, tokens_student), inner(panel_teacher, toke...  11.1 us
    dot_general x2, matrix products, inner(): jnp.einsum('rd,cd->rc', left, right, preferred_element_type=jnp.float32)  8.71 us
  transfers between devices with their start and end apart: 3, of which 3 were waited for; matrix products, arithmetic and copies ran while one was open for 5% of the time, Pallas kernels for 0%

commit v1 on v0

--- a/solution.py
+++ b/solution.py
@@ -50,7 +50,7 @@
         lax.psum_scatter(loss_part, "col", scatter_dimension=0, tiled=True),
     )
     token_part = jnp.einsum("rc,rd->cd", doubled, panel_half, preferred_element_type=jnp.float32)
-    token_term = lax.psum(token_part, "row")
+    token_term = jnp.sum(lax.all_gather(token_part, "row"), axis=0)
     share = panel_student.shape[0] // lax.axis_size("col")
     offset = lax.axis_index("col") * share
     unit_rows = lax.dynamic_slice_in_dim(panel_unit, offset, share, 0)

time: 405 us -> 509 us (1.26)
  waiting for transfers between devices: 272 us -> 362 us
  other arithmetic: 24.2 us -> 36 us
    all_gather x0 -> x1, waiting for transfers between devices: none -> 222 us  [local(): token_term = jnp.sum(lax.all_gather(token_part, 'row'), axis=0)]
    reduce_scatter x1, waiting for transfers between devices: 124 us -> 54.6 us  [local(): lax.psum_scatter(panel_part, 'col', scatter_dimension=0, tiled=True)]
    psum x1 -> x0, waiting for transfers between devices: 63.3 us -> none  [local(): token_term = lax.psum(token_part, 'row')]
    reduce_sum x0 -> x1, other arithmetic: none -> 12.5 us  [local(): token_term = jnp.sum(lax.all_gather(token_part, 'row'), axis=0)]
  transfers between devices with their start and end apart: 3 -> 3, of which waited for: 3 -> 3; matrix products, arithmetic and copies ran while one was open for 5% -> 4% of each run, Pallas kernels for 0% -> 0%
where the time goes in v1:
time: 509 us; the launch traced here: 508 us
  waiting for transfers between devices  362 us (71%)
  blocking collectives  73.4 us (14%)
  other arithmetic  36 us (7%)
  matrix products  19.3 us (4%)
  between operations  14.5 us (3%)
    all_gather x1, waiting for transfers between devices, local(): token_term = jnp.sum(lax.all_gather(token_part, 'row'), axis=0)  222 us
    psum x1, waiting for transfers between devices, local(): lax.psum((inner(panel_student, tokens_student), inner(panel_teacher, toke...  85 us
    unnamed x1, blocking collectives  55.8 us
    reduce_scatter x1, waiting for transfers between devices, local(): lax.psum_scatter(panel_part, 'col', scatter_dimension=0, tiled=True)  54.6 us
    reduce_sum x1, other arithmetic, local(): token_term = jnp.sum(lax.all_gather(token_part, 'row'), axis=0)  12.5 us
    psum x1, blocking collectives, local(): lax.psum((inner(panel_student, tokens_student), inner(panel_teacher, toke...  11.1 us
  transfers between devices with their start and end apart: 3, of which 3 were waited for; matrix products, arithmetic and copies ran while one was open for 4% of the time, Pallas kernels for 0%

profile of v1, /device:TPU:8, one launch (start us, length us, event | category | flops | bytes accessed | tf_op | source)
XLA Modules:
  0.0 508.4 jit_solution(18312923789142842105)
XLA Ops:
  7.2 0.0 copy-start
  7.2 0.0 all-reduce.6.cloned.1.call-start
  7.2 0.0 copy-start.1
  7.2 5.6 %fusion.17 = f32[512,768]{1,0:T(8,128)} fusion(bf16[512,2048]{1,0:T(8,128)(2,1)} %param.5, bf16[768,2048]{1,0:T(8,128)(2,1)} %param.7), kind=kOutput, calls=%fused_computation.31 | convolution fusion | flops 1610612736 | bytes 6815744 | tf_op jit(solution)/shard_map/rd,cd->rc/dot_general | solution.py:15
  12.9 0.0 copy-done
  12.9 0.0 copy-done.1
  12.9 3.1 fusion.16
  15.9 0.0 all-reduce.6.cloned.1.call-update
  16.0 0.0 reduce-scatter.2.cloned.1.call-start
  16.0 0.0 copy-start.2
  16.0 2.2 multiply_reduce_fusion.1
  18.3 0.0 copy-done.2
  18.3 0.5 fusion.8
  18.7 2.6 multiply_reduce_fusion
  21.3 0.7 fusion.7
  22.0 11.1 %all-reduce.2 = (f32[768]{0:T(1024)S(1)}, f32[512]{0:T(512)S(1)}, f32[768]{0:T(1024)S(1)}, f32[512]{0:T(512)S(1)}) all-reduce(f32[768]{0:T(1024)S(1)} %multiply_reduce_fusion, f32[512]{0:T(512)S(1)} %multiply_reduce_fusion.1, f32[768]{0:T(1024)S(1)} %fusion.7, f32[512]{0:T(512)S(1)} %fusion.8), channel_id=1, replica_groups=mesh['row'=4,'col'=32,'feat'=2] {'feat'}, use_global_device_ids=true, to_apply=%region_9.0 | all-reduce | flops 2560 | bytes 20480 | tf_op jit(solution)/shard_map/psum | solution.py:23
  33.1 85.0 %all-reduce.6.cloned.1.call-done = (f32[512,768]{1,0:T(8,128)}, f32[512,768]{1,0:T(8,128)}) async-done(((f32[512,768]{1,0:T(8,128)}, f32[512,768]{1,0:T(8,128)}), (f32[512,768]{1,0:T(8,128)}, f32[512,768]{1,0:T(8,128)})) %all-reduce.6.cloned.1.call-update) | async-done | bytes 3145744 | tf_op jit(solution)/shard_map/psum | solution.py:23
  118.2 2.5 multiply_reduce_fusion.2
  120.6 0.0 copy-start.3
  120.6 1.1 copy-done.3
  121.8 3.9 fusion.9
  125.7 0.0 reduce-scatter.2.cloned.1.call-update
  125.7 0.0 all-gather.3.cloned.1.call-start
  125.7 6.7 %fusion.12 = f32[768,2048]{1,0:T(8,128)} fusion(f32[512,768]{1,0:T(8,128)} %copy-done.3, bf16[512,2048]{1,0:T(8,128)(2,1)} %param.4, f32[512]{0:T(512)S(1)} %get-tuple-element.16), kind=kOutput, calls=%fused_computation.17 | convolution fusion | flops 1614544896 | bytes 9963520 | tf_op jit(solution)/shard_map/rc,rd->cd/dot_general | solution.py:52
  132.5 0.0 copy-start.5
  132.5 0.0 all-gather.3.cloned.1.call-update
  132.5 0.1 dynamic_slice.7
  132.6 0.6 copy-done.5
  133.1 0.6 dynamic-slice
  134.4 3.9 convert_multiply_fusion.2
  138.3 55.8 %all-reduce = f32[512]{0:T(512)S(1)} all-reduce(f32[512]{0:T(512)S(1)} %get-tuple-element.11), channel_id=3, replica_groups=mesh['row'=4,'col'=32,'feat'=2] {'col'}, use_global_device_ids=true, to_apply=%region_11.0.clone | all-reduce | flops 512 | bytes 4096
  194.1 0.6 dynamic-slice.1
  194.7 54.6 %reduce-scatter.2.cloned.1.call-done = f32[16,2048]{1,0:T(8,128)} async-done(((f32[512,2048]{1,0:T(8,128)}), f32[16,2048]{1,0:T(8,128)}) %reduce-scatter.2.cloned.1.call-update) | async-done | bytes 131088 | tf_op jit(solution)/shard_map/reduce_scatter | solution.py:49
  249.3 1.1 multiply_reduce_fusion.3
  250.4 222.4 %all-gather.3.cloned.1.call-done = f32[3072,2048]{1,0:T(8,128)} async-done(((f32[768,2048]{1,0:T(8,128)}), f32[3072,2048]{1,0:T(8,128)}) %all-gather.3.cloned.1.call-update) | async-done | bytes 25165840 | tf_op jit(solution)/shard_map/all_gather | solution.py:53
  472.8 12.5 %reduce_sum.78 = f32[768,2048]{1,0:T(8,128)} reduce(f32[4,768,2048]{2,1,0:T(8,128)} %bitcast.6, f32[]{:T(128)} %constant.8.clone.1), dimensions={0}, to_apply=%region_15.0 | reduce | flops 4718592 | bytes 31457284 | tf_op jit(solution)/shard_map/reduce_sum | solution.py:53
  485.3 3.7 fusion.3
  489.0 6.5 %all-reduce.1 = (f32[16]{0:T(128)S(1)}, f32[768]{0:T(1024)S(1)}) all-reduce(f32[16]{0:T(128)S(1)} %multiply_reduce_fusion.3, f32[768]{0:T(1024)S(1)} %fusion.3), channel_id=1, replica_groups=mesh['row'=4,'col'=32,'feat'=2] {'feat'}, use_global_device_ids=true, to_apply=%region_14.0 | all-reduce | flops 784 | bytes 6272 | tf_op jit(solution)/shard_map/psum | solution.py:58
  495.5 0.0 copy-start.4
  495.5 4.7 fusion.6
  500.2 0.0 copy-done.4
  500.2 1.6 multiply_convert_fusion.3
  (2 shorter events, 0.0 us)
Async XLA Ops:
  7.2 5.7 %copy-start = (bf16[768,2048]{1,0:T(8,128)(2,1)S(1)}, bf16[768,2048]{1,0:T(8,128)(2,1)}, u32[]{:S(2)}) copy-start(bf16[768,2048]{1,0:T(8,128)(2,1)} %param.6) | copy-start | bytes 9437188
  7.2 111.0 %all-reduce.6.cloned.1.call-start = ((), (), s32[]{:S(2)}) async-start(), calls=%async_computation.3 | async-start | bytes 6291456 | tf_op jit(solution)/shard_map/psum | solution.py:23
  7.2 5.7 %copy-start.1 = (bf16[512,2048]{1,0:T(8,128)(2,1)S(1)}, bf16[512,2048]{1,0:T(8,128)(2,1)}, u32[]{:S(2)}) copy-start(bf16[512,2048]{1,0:T(8,128)(2,1)} %param.4) | copy-start | bytes 6291460
  16.0 233.4 %reduce-scatter.2.cloned.1.call-start = ((), (), s32[]{:S(2)}) async-start(), calls=%async_computation.1 | async-start | bytes 4325376 | tf_op jit(solution)/shard_map/reduce_scatter | solution.py:49
  16.0 2.2 copy-start.2
  120.6 1.1 copy-start.3
  125.7 347.1 %all-gather.3.cloned.1.call-start = ((), (), s32[]{:S(2)}) async-start(), calls=%async_computation.2 | async-start | bytes 31457280 | tf_op jit(solution)/shard_map/all_gather | solution.py:53
  132.5 0.7 copy-start.5
  495.5 4.7 copy-start.4
Sparse Core Ops, SparseCore 0:
  16.1 102.0 all-reduce.5
  125.8 123.4 reduce-scatter.1
  251.1 221.5 all-gather.2
